TPU v7x, 256 devices: a whole 4x4x8 slice. The times are simulated.
256 devices in a mesh: dp: 16 (over x, y_hi, core), zero: 16 (over y_lo, z).
Axes of the slice: x: 4, y: 4 (y_hi: 2, y_lo: 2; y = y_hi * 2 + y_lo), z: 8, core: 2. Of those that a mesh axis runs over, the one named last changes fastest.
Arguments:
- picture_embeds: bfloat16 [32768, 1024], P(('dp', 'zero')), may hold values from -4 to 4
- matched_slot: int32 [32768], P(('dp', 'zero')), may hold values from 0 to 2047, as said below
- summary_token_states: bfloat16 [32768, 1024], P(('dp', 'zero')), may hold values from -10 to 10
- feedforward_inner_activations: bfloat16 [32768, 4096], P(('dp', 'zero')), may hold values from -24 to 24
- closing_layernorm_multiplier: float32 [1024], replicated, may hold values from 0.1 to 1.9
- contracting_matrix: bfloat16 [4096, 1024], P('zero'), may hold values from -0.09375 to 0.09375
- sharpness_factor: float32 [1], replicated, may hold values from 3 to 6
- additive_shift_learned: float32 [1], replicated, may hold values from -3 to -1
Outputs:
- image_grad: float32 [32768, 1024], P(('dp', 'zero'))
- hidden_grad: bfloat16 [32768, 4096], P(('dp', 'zero'))
- down_grad: float32 [4096, 1024], P('zero', 'dp')
Inputs may be any that keep to these rules, and one draw needn't show every extreme that they name: `matched_slot`: within the 2048 images of one zero index every position 0 to 2047 is named exactly once.
All inputs are finite; a program needn't handle non-finite values.
Results may differ from a plain program's by a relative error of at most 0.005.
Values may be sent and summed in bfloat16 or wider, within the bound.
A program may use at most 128 MiB of HBM per device.

v0:
```python
import jax
import jax.numpy as jnp
from jax import lax
from jax.sharding import PartitionSpec as P


def unit_rows(values):
    return values * lax.rsqrt(jnp.sum(values * values, axis=1, keepdims=True) + 1e-06)


def text_embed(features, closing_layernorm_multiplier):
    center = features - jnp.mean(features, axis=1, keepdims=True)
    spread = jnp.mean(center * center, axis=1, keepdims=True)
    return unit_rows(center * lax.rsqrt(spread + 1e-05) * closing_layernorm_multiplier)


def sigmoid_weights(scores, labels):
    return (-labels * jax.nn.sigmoid(-labels * scores)).astype(jnp.bfloat16)


def shards(
    picture_embeds,
    matched_slot,
    summary_token_states,
    feedforward_inner_activations,
    closing_layernorm_multiplier,
    contracting_matrix,
    sharpness_factor,
    additive_shift_learned,
):
    similarity_multiplier = sharpness_factor[0]
    shift_value = additive_shift_learned[0]
    local_rows, width = picture_embeds.shape
    dp_size = lax.axis_size("dp")
    zero_size = lax.axis_size("zero")
    dp_place = lax.axis_index("dp")
    own_start = dp_place * local_rows
    transpose_route = [
        (a * zero_size + b, b * zero_size + a) for a in range(dp_size) for b in range(zero_size)
    ]
    ffa_cols = lax.all_to_all(
        feedforward_inner_activations, "dp", split_axis=1, concat_axis=0, tiled=True
    )
    weight_block = lax.ppermute(contracting_matrix, ("dp", "zero"), transpose_route)
    digits = jnp.zeros((local_rows, 128), jnp.bfloat16)
    digits = digits.at[:, 0].set((matched_slot // 256).astype(jnp.bfloat16))
    digits = digits.at[:, 1].set((matched_slot % 256).astype(jnp.bfloat16))
    both = jnp.concatenate([picture_embeds, summary_token_states, digits], axis=1)
    both_g = lax.all_gather(both, "dp", axis=0, tiled=True)
    ffa_cols, weight_block, both_g = lax.optimization_barrier((ffa_cols, weight_block, both_g))
    slot_g = both_g[:, 2 * width].astype(jnp.int32) * 256 + both_g[:, 2 * width + 1].astype(
        jnp.int32
    )
    image_b_g = unit_rows(both_g[:, :width].astype(jnp.float32)).astype(jnp.bfloat16)
    caption_g, caption_back = jax.vjp(
        lambda feats: text_embed(feats, closing_layernorm_multiplier),
        both_g[:, width : 2 * width].astype(jnp.float32),
    )
    caption_b_g = caption_g.astype(jnp.bfloat16)
    group_rows = caption_b_g.shape[0]
    unit_image, image_back = jax.vjp(unit_rows, picture_embeds.astype(jnp.float32))
    scores = (
        similarity_multiplier
        * lax.dot_general(
            image_b_g, caption_b_g, (((1,), (1,)), ((), ())), preferred_element_type=jnp.float32
        )
        + shift_value
    )
    places = jnp.arange(group_rows, dtype=jnp.int32)
    labels = jnp.where(slot_g[:, None] == places[None, :], 1.0, -1.0)
    weights = sigmoid_weights(scores, labels)
    own_weights = lax.dynamic_slice_in_dim(weights, own_start, local_rows, axis=0)
    image_term = similarity_multiplier * jnp.dot(
        own_weights, caption_b_g, preferred_element_type=jnp.float32
    )
    caption_term = similarity_multiplier * lax.dot_general(
        weights, image_b_g, (((0,), (0,)), ((), ())), preferred_element_type=jnp.float32
    )
    image_grad = image_back(image_term)[0]
    upstream_g = caption_back(caption_term)[0].astype(jnp.bfloat16)
    hidden_part = lax.dot_general(
        upstream_g, weight_block, (((1,), (1,)), ((), ())), preferred_element_type=jnp.float32
    ).astype(jnp.bfloat16)
    hidden_grad = lax.all_to_all(hidden_part, "dp", split_axis=0, concat_axis=1, tiled=True)
    group_sum = lax.dot_general(
        ffa_cols, upstream_g, (((0,), (0,)), ((), ())), preferred_element_type=jnp.float32
    )
    down_parts = lax.all_to_all(group_sum, "zero", split_axis=1, concat_axis=0, tiled=True)
    down_block = jnp.sum(down_parts.reshape((zero_size,) + (group_sum.shape[0], -1)), axis=0)
    down_grad = lax.ppermute(down_block, ("dp", "zero"), transpose_route)
    return (image_grad, hidden_grad, down_grad)


def solution(mesh):
    placed = (
        P(("dp", "zero"), None),
        P(("dp", "zero")),
        P(("dp", "zero"), None),
        P(("dp", "zero"), None),
        P(),
        P("zero", None),
        P(),
        P(),
    )
    return jax.shard_map(
        shards,
        mesh=mesh,
        in_specs=placed,
        out_specs=(P(("dp", "zero"), None), P(("dp", "zero"), None), P("zero", "dp")),
        check_vma=False,
    )
```

profile of v0, /device:TPU:1, one launch (start us, length us, event | category | flops | bytes accessed | tf_op | source)
XLA Modules:
  0.0 254.7 jit_solution(212489842081570415)
XLA Ops:
  7.2 0.0 all-gather.2.cloned.1.call-start
  7.2 0.6 compare_reduce_fusion.1
  7.8 0.6 compare_reduce_fusion
  8.5 1.1 copy.21
  9.6 0.0 copy-start.3
  9.6 1.1 copy.20
  10.8 2.0 fusion.26
  12.8 0.9 pad_maximum_fusion
  13.7 0.0 all-gather.2.cloned.1.call-update
  13.7 2.3 copy.18
  16.0 8.4 %all-to-all-start = ((bf16[128,16,256]{0,2,1:T(8,128)(2,1)}), bf16[128,16,256]{0,2,1:T(8,128)(2,1)S(1)}, u32[]{:S(2)}, u32[]{:S(2)}) async-start(bf16[128,16,256]{0,2,1:T(8,128)(2,1)} %bitcast.1), calls=%async_computation | async-start | bytes 2097152 | tf_op jit(solution)/shard_map/all_to_all | solution.py:41
  24.4 3.5 %collective-permute-start = (bf16[256,1024]{1,0:T(8,128)(2,1)}, bf16[256,1024]{1,0:T(8,128)(2,1)S(1)}, u32[]{:S(2)}, u32[]{:S(2)}) collective-permute-start(bf16[256,1024]{1,0:T(8,128)(2,1)} %param.17), channel_id=1, source_target_pairs={{0,0},{1,16},{2,32},{3,48},{4,64},{5,80},{6,96},{7,112},{8,128},{9... | collective-permute-start | bytes 1572872 | tf_op jit(solution)/shard_map/ppermute | solution.py:44
  29.3 34.6 %all-to-all-done = bf16[128,16,256]{0,2,1:T(8,128)(2,1)S(1)} async-done(((bf16[128,16,256]{0,2,1:T(8,128)(2,1)}), bf16[128,16,256]{0,2,1:T(8,128)(2,1)S(1)}, u32[]{:S(2)}, u32[]{:S(2)}) %all-to-all-start) | async-done | bytes 1048608 | tf_op jit(solution)/shard_map/all_to_all | solution.py:41
  63.8 0.5 copy.19
  64.4 0.0 collective-permute-done
  64.4 69.7 %all-gather.2.cloned.1.call-done = bf16[2048,2176]{0,1:T(8,128)(2,1)} async-done(((bf16[128,2176]{0,1:T(8,128)(2,1)}), bf16[2048,2176]{0,1:T(8,128)(2,1)}) %all-gather.2.cloned.1.call-update) | async-done | bytes 8912912 | tf_op jit(solution)/shard_map/all_gather | solution.py:49
  134.1 0.0 copy-start
  134.1 3.0 %convert_reduce_fusion = f32[2048]{0:T(1024)S(1)} fusion(bf16[2048,2176]{0,1:T(8,128)(2,1)} %all-gather.2.cloned.1.call-done), kind=kLoop, calls=%fused_computation.5 | loop fusion | flops 4192256 | bytes 4202496 | tf_op jit(solution)/shard_map/jvp()/reduce_sum | solution.py:12
  137.1 1.3 convert_add_fusion
  138.4 3.3 %fusion.6 = f32[2048]{0:T(1024)S(1)} fusion(f32[2048]{0:T(1024)S(1)} %broadcast_multiply_fusion, bf16[2048,2176]{0,1:T(8,128)(2,1)} %all-gather.2.cloned.1.call-done), kind=kLoop, calls=%fused_computation.14 | loop fusion | flops 8386560 | bytes 4210688 | tf_op jit(solution)/shard_map/jvp()/reduce_sum | solution.py:13
  141.7 0.0 copy-done.3
  141.7 5.1 %fusion.12 = (f32[2048]{0:T(1024)S(1)}, f32[2048]{0:T(1024)S(1)}) fusion(f32[1024]{0:T(1024)S(1)} %copy-done.3, f32[2048]{0:T(1024)S(1)} %fusion.24, f32[2048]{0:T(1024)S(1)} %broadcast_multiply_fusion, bf16[2048,2176]{0,1:T(8,128)(2,1)} %all-gather.2.cloned.1.call-done), kind=kLoop, calls=%fused_computation.20 | loop fusion | flops 18870272 | bytes 8425472 | tf_op jit(solution)/shard_map/jvp()/reduce_sum | solution.py:8
  146.9 0.0 copy-done
  146.9 18.2 %multiply_convert_fusion = bf16[2048,2048]{1,0:T(8,128)(2,1)} fusion(f32[]{:T(128)} %bitcast.23, f32[]{:T(128)} %bitcast.19, s32[2048]{0:T(1024)S(1)} %bitcast.28, f32[2048]{0:T(1024)S(1)} %get-tuple-element.46, bf16[2048,2176]{0,1:T(8,128)(2,1)S(1)} %copy-done, f32[2048]{0:T(1024)S(1)} %get-tuple-element.47, f32[1024]{0:T(1024)S(1)} %copy-done.3, ...), kind=kOutput, calls=%fused_computation | convolution fusion | flops 8654946304 | bytes 16822280 | tf_op jit(solution)/shard_map/dot_general | solution.py:64
  165.1 11.9 %fusion.14 = (f32[2048]{0:T(1024)S(1)}, f32[2048,1024]{0,1:T(8,128)S(1)}) fusion(f32[]{:T(128)} %bitcast.22, f32[1024]{0:T(1024)S(1)} %copy-done.3, f32[2048]{0:T(1024)S(1)} %fusion.24, f32[2048]{0:T(1024)S(1)} %broadcast_multiply_fusion, bf16[2048,2176]{0,1:T(8,128)(2,1)S(1)} %copy-done, bf16[2048,2048]{1,0:T(8,128)(2,1)} %multiply_convert_fusion, ...), kind=kOutput, calls=%fused_computation.22 | convolution fusion | flops 8610904064 | bytes 25202692 | tf_op jit(solution)/shard_map/dot_general | solution.py:76
  177.0 3.9 %fusion.15 = f32[2048]{0:T(1024)S(1)} fusion(f32[2048,1024]{0,1:T(8,128)S(1)} %get-tuple-element.45, f32[2048]{0:T(1024)S(1)} %multiply_multiply_fusion.1, f32[]{:T(128)} %bitcast.21, f32[2048]{0:T(1024)S(1)} %get-tuple-element.47, f32[1024]{0:T(1024)S(1)} %copy-done.3, f32[2048]{0:T(1024)S(1)} %fusion.24, f32[2048]{0:T(1024)S(1)} %broadcast_multiply_fusion, ...), kind=kLoop, calls=%fused_computation.23 | loop fusion | flops 25163776 | bytes 12627972 | tf_op jit(solution)/shard_map/transpose(jvp())/reduce_sum | solution.py:14
  180.9 4.6 %fusion.31 = (f32[2048]{0:T(1024)S(1)}, f32[2048,1024]{0,1:T(8,128)S(1)}) fusion(f32[2048]{0:T(1024)S(1)} %multiply_multiply_fusion, f32[2048]{0:T(1024)S(1)} %multiply_multiply_fusion.1, f32[1024]{0:T(1024)S(1)} %copy-done.3, f32[2048]{0:T(1024)S(1)} %fusion.24, f32[2048]{0:T(1024)S(1)} %broadcast_multiply_fusion, bf16[2048,2176]{0,1:T(8,128)(2,1)S(1)} %copy-done, ...), kind=kLoop, calls=%fused_computation.63 | loop fusion | flops 31455232 | bytes 21024772 | tf_op jit(solution)/shard_map/transpose(jvp())/reduce_sum | solution.py:12
  185.5 0.0 copy-start.1
  185.6 2.9 %fusion.20 = f32[256,1024]{0,1:T(8,128)} fusion(bf16[2048,256]{1,0:T(8,128)(2,1)S(1)} %bitcast.26, f32[2048,1024]{0,1:T(8,128)S(1)} %get-tuple-element.38, f32[2048]{0:T(1024)S(1)} %negate_multiply_fusion), kind=kOutput, calls=%fused_computation.28 | convolution fusion | flops 1077936128 | bytes 10493952 | tf_op jit(solution)/shard_map/dot_general | solution.py:85
  188.4 0.8 copy-done.1
  189.2 6.9 %all-to-all-start.2 = ((f32[256,16,64]{0,2,1:T(8,128)}), f32[256,16,64]{0,2,1:T(8,128)S(1)}, u32[]{:S(2)}, u32[]{:S(2)}) async-start(f32[256,16,64]{0,2,1:T(8,128)} %bitcast.10), calls=%async_computation.2 | async-start | bytes 2097152 | tf_op jit(solution)/shard_map/all_to_all | solution.py:88
  196.0 0.0 copy-start.2
  196.1 5.8 %convolution_convert_fusion = bf16[2048,256]{1,0:T(8,128)(2,1)} fusion(bf16[256,1024]{1,0:T(8,128)(2,1)S(1)} %collective-permute-done, f32[2048,1024]{0,1:T(8,128)} %copy-done.1, f32[2048]{0:T(1024)S(1)} %negate_multiply_fusion), kind=kOutput, calls=%fused_computation.27 | convolution fusion | flops 1078460416 | bytes 9969664 | tf_op jit(solution)/shard_map/dot_general | solution.py:81
  201.8 19.7 %all-to-all-done.2 = f32[256,16,64]{0,2,1:T(8,128)S(1)} async-done(((f32[256,16,64]{0,2,1:T(8,128)}), f32[256,16,64]{0,2,1:T(8,128)S(1)}, u32[]{:S(2)}, u32[]{:S(2)}) %all-to-all-start.2) | async-done | bytes 1048608 | tf_op jit(solution)/shard_map/all_to_all | solution.py:88
  221.5 7.4 %all-to-all-start.1 = ((bf16[16,128,256]{2,1,0:T(8,128)(2,1)}), bf16[16,128,256]{2,1,0:T(8,128)(2,1)S(1)}, u32[]{:S(2)}, u32[]{:S(2)}) async-start(bf16[16,128,256]{2,1,0:T(8,128)(2,1)} %bitcast.8), calls=%async_computation.1 | async-start | bytes 2097152 | tf_op jit(solution)/shard_map/all_to_all | solution.py:84
  228.9 0.0 copy-done.2
  228.9 4.2 %fusion.21 = (f32[128]{0:T(128)S(1)}, f32[128]{0:T(128)S(1)}, f32[128,1024]{1,0:T(8,128)S(1)}) fusion(bf16[128,1024]{1,0:T(8,128)(2,1)S(1)} %copy-done.2, f32[2048]{0:T(1024)S(1)} %get-tuple-element.47, f32[1024]{0:T(1024)S(1)} %copy-done.3, f32[2048]{0:T(1024)S(1)} %fusion.24, f32[2048]{0:T(1024)S(1)} %broadcast_multiply_fusion, ...), kind=kOutput, calls=%fused_computation.35 | convolution fusion | flops 550240000 | bytes 5535236 | tf_op jit(solution)/shard_map/dot_general | solution.py:73
  233.2 0.1 reduce_sum.115
  233.2 2.7 %collective-permute-start.1 = (f32[256,64]{0,1:T(8,128)S(1)}, f32[256,64]{0,1:T(8,128)S(1)}, u32[]{:S(2)}, u32[]{:S(2)}) collective-permute-start(f32[256,64]{0,1:T(8,128)S(1)} %reduce_sum.115), channel_id=1, source_target_pairs={{0,0},{1,16},{2,32},{3,48},{4,64},{5,80},{6,96},{7,112},{8,128},{9... | collective-permute-start | bytes 196616 | tf_op jit(solution)/shard_map/ppermute | solution.py:90
  236.0 1.0 add_add_fusion.2
  236.9 9.2 %all-to-all-done.1 = bf16[16,128,256]{2,1,0:T(8,128)(2,1)S(1)} async-done(((bf16[16,128,256]{2,1,0:T(8,128)(2,1)}), bf16[16,128,256]{2,1,0:T(8,128)(2,1)S(1)}, u32[]{:S(2)}, u32[]{:S(2)}) %all-to-all-start.1) | async-done | bytes 1048608 | tf_op jit(solution)/shard_map/all_to_all | solution.py:84
  246.1 1.1 copy.25
  247.2 0.0 collective-permute-done.1
  247.2 0.6 copy.30
  (9 shorter events, 0.1 us)
Async XLA Ops:
  7.2 126.9 %all-gather.2.cloned.1.call-start = ((), (), s32[]{:S(2)}) async-start(), calls=%async_computation.3 | async-start | bytes 9469952 | tf_op jit(solution)/shard_map/all_gather | solution.py:49
  9.6 132.1 %copy-start.3 = (f32[1024]{0:T(1024)S(1)}, f32[1024]{0:T(1024)}, u32[]{:S(2)}) copy-start(f32[1024]{0:T(1024)} %param.16) | copy-start | bytes 12292
  16.0 47.8 %all-to-all-start = ((bf16[128,16,256]{0,2,1:T(8,128)(2,1)}), bf16[128,16,256]{0,2,1:T(8,128)(2,1)S(1)}, u32[]{:S(2)}, u32[]{:S(2)}) async-start(bf16[128,16,256]{0,2,1:T(8,128)(2,1)} %bitcast.1), calls=%async_computation | async-start | bytes 2097152 | tf_op jit(solution)/shard_map/all_to_all | solution.py:41
  24.4 39.9 %collective-permute-start = (bf16[256,1024]{1,0:T(8,128)(2,1)}, bf16[256,1024]{1,0:T(8,128)(2,1)S(1)}, u32[]{:S(2)}, u32[]{:S(2)}) collective-permute-start(bf16[256,1024]{1,0:T(8,128)(2,1)} %param.17), channel_id=1, source_target_pairs={{0,0},{1,16},{2,32},{3,48},{4,64},{5,80},{6,96},{7,112},{8,128},{9... | collective-permute-start | bytes 1572872 | tf_op jit(solution)/shard_map/ppermute | solution.py:44
  134.1 12.8 %copy-start = (bf16[2048,2176]{0,1:T(8,128)(2,1)S(1)}, bf16[2048,2176]{0,1:T(8,128)(2,1)}, u32[]{:S(2)}) copy-start(bf16[2048,2176]{0,1:T(8,128)(2,1)} %all-gather.2.cloned.1.call-done) | copy-start | bytes 26738692
  185.5 3.6 %copy-start.1 = (f32[2048,1024]{0,1:T(8,128)}, f32[2048,1024]{0,1:T(8,128)S(1)}, u32[]{:S(2)}) copy-start(f32[2048,1024]{0,1:T(8,128)S(1)} %get-tuple-element.38) | copy-start | bytes 25165828
  189.2 32.3 %all-to-all-start.2 = ((f32[256,16,64]{0,2,1:T(8,128)}), f32[256,16,64]{0,2,1:T(8,128)S(1)}, u32[]{:S(2)}, u32[]{:S(2)}) async-start(f32[256,16,64]{0,2,1:T(8,128)} %bitcast.10), calls=%async_computation.2 | async-start | bytes 2097152 | tf_op jit(solution)/shard_map/all_to_all | solution.py:88
  196.0 32.9 %copy-start.2 = (bf16[128,1024]{1,0:T(8,128)(2,1)S(1)}, bf16[128,1024]{1,0:T(8,128)(2,1)}, u32[]{:S(2)}) copy-start(bf16[128,1024]{1,0:T(8,128)(2,1)} %param.12) | copy-start | bytes 786436
  221.5 24.6 %all-to-all-start.1 = ((bf16[16,128,256]{2,1,0:T(8,128)(2,1)}), bf16[16,128,256]{2,1,0:T(8,128)(2,1)S(1)}, u32[]{:S(2)}, u32[]{:S(2)}) async-start(bf16[16,128,256]{2,1,0:T(8,128)(2,1)} %bitcast.8), calls=%async_computation.1 | async-start | bytes 2097152 | tf_op jit(solution)/shard_map/all_to_all | solution.py:84
  233.2 14.0 %collective-permute-start.1 = (f32[256,64]{0,1:T(8,128)S(1)}, f32[256,64]{0,1:T(8,128)S(1)}, u32[]{:S(2)}, u32[]{:S(2)}) collective-permute-start(f32[256,64]{0,1:T(8,128)S(1)} %reduce_sum.115), channel_id=1, source_target_pairs={{0,0},{1,16},{2,32},{3,48},{4,64},{5,80},{6,96},{7,112},{8,128},{9... | collective-permute-start | bytes 196616 | tf_op jit(solution)/shard_map/ppermute | solution.py:90
Sparse Core Ops, SparseCore 0:
  13.8 120.1 all-gather.1
where the time goes:
time: 255 us
  waiting for transfers between devices  133 us (52%)
  matrix products  42.9 us (17%)
  starting transfers between devices  29 us (11%)
  other arithmetic  26.4 us (10%)
  between operations  15.5 us (6%)
  local copies, waits for them, and re-layouts  7.57 us (3%)
    all_gather x1, waiting for transfers between devices, shards(): both_g = lax.all_gather(both, 'dp', axis=0, tiled=True)  69.7 us
    all_to_all x1, waiting for transfers between devices, shards(): lax.all_to_all(feedforward_inner_activations, 'dp', split_axis=1, concat_...  34.6 us
    all_to_all x1, waiting for transfers between devices, shards(): lax.all_to_all(group_sum, 'zero', split_axis=1, concat_axis=0, tiled=True)  19.7 us
    dot_general x1, matrix products, shards(): lax.dot_general(image_b_g, caption_b_g, (((1,), (1,)), ((), ())), preferr...  18.2 us
    dot_general x1, matrix products, shards(): lax.dot_general(weights, image_b_g, (((0,), (0,)), ((), ())), preferred_e...  11.9 us
    all_to_all x1, waiting for transfers between devices, shards(): lax.all_to_all(hidden_part, 'dp', split_axis=0, concat_axis=1, tiled=True)  9.2 us
    all_to_all x1, starting transfers between devices, shards(): lax.all_to_all(feedforward_inner_activations, 'dp', split_axis=1, concat_...  8.45 us
    reduce_sum x2, other arithmetic, text_embed(): center = features - jnp.mean(features, axis=1, keepdims=True)  7.6 us
  transfers between devices with their start and end apart: 6, of which 4 were waited for; matrix products, arithmetic and copies ran while one was open for 6% of the time, Pallas kernels for 0%

commit v1 on v0

--- a/solution.py
+++ b/solution.py
@@ -85,7 +85,12 @@
     group_sum = lax.dot_general(
         ffa_cols, upstream_g, (((0,), (0,)), ((), ())), preferred_element_type=jnp.float32
     )
-    down_parts = lax.all_to_all(group_sum, "zero", split_axis=1, concat_axis=0, tiled=True)
+    down_parts = jnp.concatenate(
+        lax.all_to_all(
+            jnp.stack(jnp.split(group_sum, lax.axis_size("zero"), axis=1)), "zero", 0, 0
+        ),
+        axis=0,
+    )
     down_block = jnp.sum(down_parts.reshape((zero_size,) + (group_sum.shape[0], -1)), axis=0)
     down_grad = lax.ppermute(down_block, ("dp", "zero"), transpose_route)
     return (image_grad, hidden_grad, down_grad)

time: 255 us -> 262 us (1.027); the launches traced: 255 us -> 258 us
  local copies, waits for them, and re-layouts: 7.57 us -> 12.7 us
    unnamed x12 -> x28, local copies, waits for them, and re-layouts: 5.93 us -> 9.38 us
where the time goes in v1:
time: 262 us; the launch traced here: 258 us
  waiting for transfers between devices  133 us (51%)
  matrix products  41.4 us (16%)
  starting transfers between devices  29.1 us (11%)
  other arithmetic  26.4 us (10%)
  between operations  15.7 us (6%)
  local copies, waits for them, and re-layouts  12.7 us (5%)
    all_gather x1, waiting for transfers between devices, shards(): both_g = lax.all_gather(both, 'dp', axis=0, tiled=True)  69.7 us
    all_to_all x1, waiting for transfers between devices, shards(): lax.all_to_all(feedforward_inner_activations, 'dp', split_axis=1, concat_...  34.6 us
    all_to_all x1, waiting for transfers between devices, shards(): lax.all_to_all(jnp.stack(jnp.split(group_sum, lax.axis_size('zero'), axis...  19.6 us
    dot_general x1, matrix products, shards(): lax.dot_general(image_b_g, caption_b_g, (((1,), (1,)), ((), ())), preferr...  18.2 us
    dot_general x1, matrix products, shards(): lax.dot_general(weights, image_b_g, (((0,), (0,)), ((), ())), preferred_e...  11.9 us
    unnamed x28, local copies, waits for them, and re-layouts  9.38 us
    all_to_all x1, waiting for transfers between devices, shards(): lax.all_to_all(hidden_part, 'dp', split_axis=0, concat_axis=1, tiled=True)  9.11 us
    all_to_all x1, starting transfers between devices, shards(): lax.all_to_all(feedforward_inner_activations, 'dp', split_axis=1, concat_...  8.45 us
  transfers between devices with their start and end apart: 6, of which 4 were waited for; matrix products, arithmetic and copies ran while one was open for 6% of the time, Pallas kernels for 0%

profile of v1, /device:TPU:1, one launch (start us, length us, event | category | flops | bytes accessed | tf_op | source)
XLA Modules:
  0.0 258.3 jit_solution(12395940702288194713)
XLA Ops:
  7.2 0.0 all-gather.2.cloned.1.call-start
  7.2 0.6 compare_reduce_fusion.1
  7.8 0.6 compare_reduce_fusion
  8.5 1.1 copy.25
  9.6 0.0 copy-start.3
  9.6 1.1 copy.24
  10.8 2.0 fusion.42
  12.8 0.9 pad_maximum_fusion
  13.7 0.0 all-gather.2.cloned.1.call-update
  13.7 2.3 copy.22
  16.0 8.4 %all-to-all-start = ((bf16[128,16,256]{0,2,1:T(8,128)(2,1)}), bf16[128,16,256]{0,2,1:T(8,128)(2,1)S(1)}, u32[]{:S(2)}, u32[]{:S(2)}) async-start(bf16[128,16,256]{0,2,1:T(8,128)(2,1)} %bitcast.1), calls=%async_computation | async-start | bytes 2097152 | tf_op jit(solution)/shard_map/all_to_all | solution.py:41
  24.4 3.5 %collective-permute-start = (bf16[256,1024]{1,0:T(8,128)(2,1)}, bf16[256,1024]{1,0:T(8,128)(2,1)S(1)}, u32[]{:S(2)}, u32[]{:S(2)}) collective-permute-start(bf16[256,1024]{1,0:T(8,128)(2,1)} %param.17), channel_id=1, source_target_pairs={{0,0},{1,16},{2,32},{3,48},{4,64},{5,80},{6,96},{7,112},{8,128},{9... | collective-permute-start | bytes 1572872 | tf_op jit(solution)/shard_map/ppermute | solution.py:44
  29.3 34.6 %all-to-all-done = bf16[128,16,256]{0,2,1:T(8,128)(2,1)S(1)} async-done(((bf16[128,16,256]{0,2,1:T(8,128)(2,1)}), bf16[128,16,256]{0,2,1:T(8,128)(2,1)S(1)}, u32[]{:S(2)}, u32[]{:S(2)}) %all-to-all-start) | async-done | bytes 1048608 | tf_op jit(solution)/shard_map/all_to_all | solution.py:41
  63.8 0.5 copy.23
  64.3 0.0 collective-permute-done
  64.3 69.7 %all-gather.2.cloned.1.call-done = bf16[2048,2176]{0,1:T(8,128)(2,1)} async-done(((bf16[128,2176]{0,1:T(8,128)(2,1)}), bf16[2048,2176]{0,1:T(8,128)(2,1)}) %all-gather.2.cloned.1.call-update) | async-done | bytes 8912912 | tf_op jit(solution)/shard_map/all_gather | solution.py:49
  134.1 3.0 %convert_reduce_fusion = f32[2048]{0:T(1024)S(1)} fusion(bf16[2048,2176]{0,1:T(8,128)(2,1)} %all-gather.2.cloned.1.call-done), kind=kLoop, calls=%fused_computation.5 | loop fusion | flops 4192256 | bytes 4202496 | tf_op jit(solution)/shard_map/jvp()/reduce_sum | solution.py:12
  137.1 1.3 convert_add_fusion
  138.4 3.3 %fusion.6 = f32[2048]{0:T(1024)S(1)} fusion(f32[2048]{0:T(1024)S(1)} %broadcast_multiply_fusion, bf16[2048,2176]{0,1:T(8,128)(2,1)} %all-gather.2.cloned.1.call-done), kind=kLoop, calls=%fused_computation.14 | loop fusion | flops 8386560 | bytes 4210688 | tf_op jit(solution)/shard_map/jvp()/reduce_sum | solution.py:13
  141.7 5.1 %fusion.12 = (f32[2048]{0:T(1024)S(1)}, f32[2048]{0:T(1024)S(1)}) fusion(f32[1024]{0:T(1024)S(1)} %copy-done.3, f32[2048]{0:T(1024)S(1)} %fusion.40, f32[2048]{0:T(1024)S(1)} %broadcast_multiply_fusion, bf16[2048,2176]{0,1:T(8,128)(2,1)} %all-gather.2.cloned.1.call-done), kind=kLoop, calls=%fused_computation.20 | loop fusion | flops 18870272 | bytes 8425472 | tf_op jit(solution)/shard_map/jvp()/reduce_sum | solution.py:8
  146.9 18.2 %multiply_convert_fusion = bf16[2048,2048]{1,0:T(8,128)(2,1)} fusion(f32[]{:T(128)} %bitcast.86, f32[]{:T(128)} %bitcast.82, s32[2048]{0:T(1024)S(1)} %bitcast.91, f32[2048]{0:T(1024)S(1)} %get-tuple-element.49, bf16[2048,2176]{0,1:T(8,128)(2,1)S(1)} %copy-done, f32[2048]{0:T(1024)S(1)} %get-tuple-element.50, f32[1024]{0:T(1024)S(1)} %copy-done.3, ...), kind=kOutput, calls=%fused_computation | convolution fusion | flops 8654946304 | bytes 16822280 | tf_op jit(solution)/shard_map/dot_general | solution.py:64
  165.1 11.9 %fusion.14 = (f32[2048]{0:T(1024)S(1)}, f32[2048,1024]{0,1:T(8,128)S(1)}) fusion(f32[]{:T(128)} %bitcast.85, f32[1024]{0:T(1024)S(1)} %copy-done.3, f32[2048]{0:T(1024)S(1)} %fusion.40, f32[2048]{0:T(1024)S(1)} %broadcast_multiply_fusion, bf16[2048,2176]{0,1:T(8,128)(2,1)S(1)} %copy-done, bf16[2048,2048]{1,0:T(8,128)(2,1)} %multiply_convert_fusion, ...), kind=kOutput, calls=%fused_computation.22 | convolution fusion | flops 8610904064 | bytes 25202692 | tf_op jit(solution)/shard_map/dot_general | solution.py:76
  177.0 3.9 %fusion.15 = f32[2048]{0:T(1024)S(1)} fusion(f32[2048,1024]{0,1:T(8,128)S(1)} %get-tuple-element.48, f32[2048]{0:T(1024)S(1)} %multiply_multiply_fusion.1, f32[]{:T(128)} %bitcast.84, f32[2048]{0:T(1024)S(1)} %get-tuple-element.50, f32[1024]{0:T(1024)S(1)} %copy-done.3, f32[2048]{0:T(1024)S(1)} %fusion.40, f32[2048]{0:T(1024)S(1)} %broadcast_multiply_fusion, ...), kind=kLoop, calls=%fused_computation.23 | loop fusion | flops 25163776 | bytes 12627972 | tf_op jit(solution)/shard_map/transpose(jvp())/reduce_sum | solution.py:14
  180.9 4.6 %fusion.47 = (f32[2048]{0:T(1024)S(1)}, f32[2048,1024]{0,1:T(8,128)S(1)}) fusion(f32[2048]{0:T(1024)S(1)} %multiply_multiply_fusion, f32[2048]{0:T(1024)S(1)} %multiply_multiply_fusion.1, f32[1024]{0:T(1024)S(1)} %copy-done.3, f32[2048]{0:T(1024)S(1)} %fusion.40, f32[2048]{0:T(1024)S(1)} %broadcast_multiply_fusion, bf16[2048,2176]{0,1:T(8,128)(2,1)S(1)} %copy-done, ...), kind=kLoop, calls=%fused_computation.95 | loop fusion | flops 31455232 | bytes 21024772 | tf_op jit(solution)/shard_map/transpose(jvp())/reduce_sum | solution.py:12
  185.5 3.2 %copy-done.1 = f32[2048,1024]{0,1:T(8,128)} copy-done((f32[2048,1024]{0,1:T(8,128)}, f32[2048,1024]{0,1:T(8,128)S(1)}, u32[]{:S(2)}) %copy-start.1) | copy-done | bytes 8388632
  188.8 1.3 fusion.20
  190.1 0.1 fusion.38
  190.3 0.1 fusion.36
  190.4 0.1 fusion.34
  190.5 0.1 fusion.32
  190.7 0.1 fusion.30
  190.8 0.1 fusion.28
  190.9 0.1 fusion.26
  191.0 0.1 fusion.24
  191.1 1.6 copy.27
  192.8 6.9 %all-to-all-start.2 = ((f32[16,256,64]{1,2,0:T(8,128)}), f32[16,256,64]{1,2,0:T(8,128)S(1)}, u32[]{:S(2)}, u32[]{:S(2)}) async-start(f32[16,256,64]{1,2,0:T(8,128)} %copy.27), calls=%async_computation.2 | async-start | bytes 2097152 | tf_op jit(solution)/shard_map/all_to_all | solution.py:89
  199.6 0.0 copy-start.2
  199.6 5.8 %convolution_convert_fusion = bf16[2048,256]{1,0:T(8,128)(2,1)} fusion(bf16[256,1024]{1,0:T(8,128)(2,1)S(1)} %collective-permute-done, f32[2048,1024]{0,1:T(8,128)} %copy-done.1, f32[2048]{0:T(1024)S(1)} %negate_multiply_fusion), kind=kOutput, calls=%fused_computation.27 | convolution fusion | flops 1078460416 | bytes 9969664 | tf_op jit(solution)/shard_map/dot_general | solution.py:81
  205.4 19.6 %all-to-all-done.2 = f32[16,256,64]{1,2,0:T(8,128)S(1)} async-done(((f32[16,256,64]{1,2,0:T(8,128)}), f32[16,256,64]{1,2,0:T(8,128)S(1)}, u32[]{:S(2)}, u32[]{:S(2)}) %all-to-all-start.2) | async-done | bytes 1048608 | tf_op jit(solution)/shard_map/all_to_all | solution.py:89
  225.0 7.5 %all-to-all-start.1 = ((bf16[16,128,256]{2,1,0:T(8,128)(2,1)}), bf16[16,128,256]{2,1,0:T(8,128)(2,1)S(1)}, u32[]{:S(2)}, u32[]{:S(2)}) async-start(bf16[16,128,256]{2,1,0:T(8,128)(2,1)} %bitcast.8), calls=%async_computation.1 | async-start | bytes 2097152 | tf_op jit(solution)/shard_map/all_to_all | solution.py:84
  232.5 4.2 %fusion.21 = (f32[128]{0:T(128)S(1)}, f32[128]{0:T(128)S(1)}, f32[128,1024]{1,0:T(8,128)S(1)}) fusion(bf16[128,1024]{1,0:T(8,128)(2,1)S(1)} %copy-done.2, f32[2048]{0:T(1024)S(1)} %get-tuple-element.50, f32[1024]{0:T(1024)S(1)} %copy-done.3, f32[2048]{0:T(1024)S(1)} %fusion.40, f32[2048]{0:T(1024)S(1)} %broadcast_multiply_fusion, ...), kind=kOutput, calls=%fused_computation.35 | convolution fusion | flops 550240000 | bytes 5535236 | tf_op jit(solution)/shard_map/dot_general | solution.py:73
  236.7 0.1 reduce_sum.115
  236.8 0.1 copy.30
  236.9 2.7 %collective-permute-start.1 = (f32[256,64]{1,0:T(8,128)S(1)}, f32[256,64]{1,0:T(8,128)S(1)}, u32[]{:S(2)}, u32[]{:S(2)}) collective-permute-start(f32[256,64]{1,0:T(8,128)S(1)} %copy.30), channel_id=1, source_target_pairs={{0,0},{1,16},{2,32},{3,48},{4,64},{5,80},{6,96},{7,112},{8,128},{9... | collective-permute-start | bytes 196616 | tf_op jit(solution)/shard_map/ppermute | solution.py:95
  239.6 0.9 add_add_fusion.2
  240.6 9.1 %all-to-all-done.1 = bf16[16,128,256]{2,1,0:T(8,128)(2,1)S(1)} async-done(((bf16[16,128,256]{2,1,0:T(8,128)(2,1)}), bf16[16,128,256]{2,1,0:T(8,128)(2,1)S(1)}, u32[]{:S(2)}, u32[]{:S(2)}) %all-to-all-start.1) | async-done | bytes 1048608 | tf_op jit(solution)/shard_map/all_to_all | solution.py:84
  249.7 1.1 copy.31
  250.8 0.7 copy.29
  (23 shorter events, 0.3 us)
Async XLA Ops:
  7.2 126.9 %all-gather.2.cloned.1.call-start = ((), (), s32[]{:S(2)}) async-start(), calls=%async_computation.3 | async-start | bytes 9469952 | tf_op jit(solution)/shard_map/all_gather | solution.py:49
  9.6 132.1 %copy-start.3 = (f32[1024]{0:T(1024)S(1)}, f32[1024]{0:T(1024)}, u32[]{:S(2)}) copy-start(f32[1024]{0:T(1024)} %param.16) | copy-start | bytes 12292
  16.0 47.8 %all-to-all-start = ((bf16[128,16,256]{0,2,1:T(8,128)(2,1)}), bf16[128,16,256]{0,2,1:T(8,128)(2,1)S(1)}, u32[]{:S(2)}, u32[]{:S(2)}) async-start(bf16[128,16,256]{0,2,1:T(8,128)(2,1)} %bitcast.1), calls=%async_computation | async-start | bytes 2097152 | tf_op jit(solution)/shard_map/all_to_all | solution.py:41
  24.4 39.9 %collective-permute-start = (bf16[256,1024]{1,0:T(8,128)(2,1)}, bf16[256,1024]{1,0:T(8,128)(2,1)S(1)}, u32[]{:S(2)}, u32[]{:S(2)}) collective-permute-start(bf16[256,1024]{1,0:T(8,128)(2,1)} %param.17), channel_id=1, source_target_pairs={{0,0},{1,16},{2,32},{3,48},{4,64},{5,80},{6,96},{7,112},{8,128},{9... | collective-permute-start | bytes 1572872 | tf_op jit(solution)/shard_map/ppermute | solution.py:44
  134.1 12.8 %copy-start = (bf16[2048,2176]{0,1:T(8,128)(2,1)S(1)}, bf16[2048,2176]{0,1:T(8,128)(2,1)}, u32[]{:S(2)}) copy-start(bf16[2048,2176]{0,1:T(8,128)(2,1)} %all-gather.2.cloned.1.call-done) | copy-start | bytes 26738692
  185.5 3.3 %copy-start.1 = (f32[2048,1024]{0,1:T(8,128)}, f32[2048,1024]{0,1:T(8,128)S(1)}, u32[]{:S(2)}) copy-start(f32[2048,1024]{0,1:T(8,128)S(1)} %get-tuple-element.41) | copy-start | bytes 25165828
  192.8 32.3 %all-to-all-start.2 = ((f32[16,256,64]{1,2,0:T(8,128)}), f32[16,256,64]{1,2,0:T(8,128)S(1)}, u32[]{:S(2)}, u32[]{:S(2)}) async-start(f32[16,256,64]{1,2,0:T(8,128)} %copy.27), calls=%async_computation.2 | async-start | bytes 2097152 | tf_op jit(solution)/shard_map/all_to_all | solution.py:89
  199.6 32.9 %copy-start.2 = (bf16[128,1024]{1,0:T(8,128)(2,1)S(1)}, bf16[128,1024]{1,0:T(8,128)(2,1)}, u32[]{:S(2)}) copy-start(bf16[128,1024]{1,0:T(8,128)(2,1)} %param.12) | copy-start | bytes 786436
  225.0 24.7 %all-to-all-start.1 = ((bf16[16,128,256]{2,1,0:T(8,128)(2,1)}), bf16[16,128,256]{2,1,0:T(8,128)(2,1)S(1)}, u32[]{:S(2)}, u32[]{:S(2)}) async-start(bf16[16,128,256]{2,1,0:T(8,128)(2,1)} %bitcast.8), calls=%async_computation.1 | async-start | bytes 2097152 | tf_op jit(solution)/shard_map/all_to_all | solution.py:84
  236.9 13.9 %collective-permute-start.1 = (f32[256,64]{1,0:T(8,128)S(1)}, f32[256,64]{1,0:T(8,128)S(1)}, u32[]{:S(2)}, u32[]{:S(2)}) collective-permute-start(f32[256,64]{1,0:T(8,128)S(1)} %copy.30), channel_id=1, source_target_pairs={{0,0},{1,16},{2,32},{3,48},{4,64},{5,80},{6,96},{7,112},{8,128},{9... | collective-permute-start | bytes 196616 | tf_op jit(solution)/shard_map/ppermute | solution.py:95
Sparse Core Ops, SparseCore 0:
  13.8 120.1 all-gather.1
